TPU v7x, 128 devices: a whole 4x4x4 slice. The times are simulated.
128 devices in a mesh: grp: 2 (over x_lo), seq: 64 (over z, x_hi, y, core).
Axes of the slice: x: 4 (x_hi: 2, x_lo: 2; x = x_hi * 2 + x_lo), y: 4, z: 4, core: 2. Of those that a mesh axis runs over, the one named last changes fastest.
Arguments:
- feats: bfloat16 [128, 128, 384], P('seq', None, 'grp'), may hold values from -6 to 6
- conv_weight: bfloat16 [3, 128, 128], replicated, may hold values from -0.3125 to 0.3125
- conv_bias: float32 [128], replicated, may hold values from -3 to 3
- latent_projection_weight: bfloat16 [16, 128], replicated, may hold values from -0.75 to 0.75
- noise: bfloat16 [128, 16, 384], P('seq', None, 'grp'), may hold values from -6 to 6
- step_index: int32 [1], replicated, may hold values from 0 to 49
- hist: bfloat16 [512, 64], P('seq'), may hold values from -6 to 6
- hist_level: int32 [512], P('seq'), may hold values from 0 to 2
- hist_count: int32 [64], replicated, may hold values from 1 to 8, 384 in all
- w_in: bfloat16 [64, 3072], replicated, may hold values from -2 to 2
- w_hist: bfloat16 [3, 64, 3072], replicated, may hold values from -0.75 to 0.75
- norm_gain: float32 [3072], replicated, may hold values from 0.5 to 2
- w_query: bfloat16 [3072, 1536], P(None, 'grp'), may hold values from -2 to 2
- w_key: bfloat16 [3072, 1536], P(None, 'grp'), may hold values from -2 to 2
- w_value: bfloat16 [3072, 1536], P(None, 'grp'), may hold values from -0.109375 to 0.109375
- q_gain: float32 [128], replicated, may hold values from 0.5 to 6
- k_gain: float32 [128], replicated, may hold values from 0.5 to 6
- w_out: bfloat16 [1536, 3072], P('grp'), may hold values from -0.5 to 0.5
Outputs:
- attention_out: bfloat16 [12288, 3072], P('seq', 'grp')
Inputs may be any that keep to these rules, and one draw needn't show every extreme that they name: hist_count[s] of the 8 history slots of seq index s are live; the largest count is exactly 8.
All inputs are finite; a program needn't handle non-finite values.
Results may differ from a plain program's by a relative error of at most 0.0095.
The roundings to bfloat16 on the way count: a program that leaves them out, or rounds other values in their place, can miss the bound.
Values may be sent and summed in bfloat16 or wider, within the bound.
A program may use at most 256 MiB of HBM per device.

v0:
```python
import math
import jax
import jax.numpy as jnp
from jax import lax
from jax.sharding import PartitionSpec as P

STEPS = 50
EPSILON = 1e-06


def from_behind(value, axis, steps):
    count = lax.axis_size(axis)
    initial, last = (max(0, -steps), min(count, count - steps))
    return lax.ppermute(value, axis, [(source, source + steps) for source in range(initial, last)])


def time_embed(step_index, width):
    half_width = width // 2
    frequency = jnp.exp(-math.log(10000.0) * jnp.arange(half_width, dtype=jnp.float32) / half_width)
    angles = step_index[0].astype(jnp.float32) * frequency
    return jnp.concatenate([jnp.cos(angles), jnp.sin(angles)])


def rms_scale(values, gain):
    return values * lax.rsqrt(jnp.mean(values * values, axis=-1, keepdims=True) + EPSILON) * gain


def local(
    feats,
    conv_weight,
    conv_bias,
    latent_projection_weight,
    noise,
    step_index,
    hist,
    hist_level,
    hist_count,
    w_in,
    w_hist,
    norm_gain,
    w_query,
    w_key,
    w_value,
    q_gain,
    k_gain,
    w_out,
):
    frame_count, channels, pixels = feats.shape
    earlier = from_behind(feats, "seq", 1)
    padded = jnp.concatenate([earlier, feats], axis=0)
    total = jnp.zeros(feats.shape, jnp.float32)
    for tap_index in range(3):
        window = padded[2 - tap_index : 2 - tap_index + frame_count]
        total = total + jnp.einsum(
            "oc,tcp->top", conv_weight[tap_index], window, preferred_element_type=jnp.float32
        )
    hidden_state = jax.nn.silu(total + conv_bias[None, :, None]).astype(jnp.bfloat16)
    sigma = (STEPS - step_index[0].astype(jnp.float32)) / STEPS
    latent_input = jnp.einsum(
        "qb,zby->zqy", latent_projection_weight, hidden_state, preferred_element_type=jnp.float32
    )
    noisy = ((1.0 - sigma) * latent_input + sigma * noise.astype(jnp.float32)).astype(jnp.bfloat16)
    lat_channels = noisy.shape[1]
    patches = (
        noisy.reshape(frame_count, lat_channels, pixels // 4, 4)
        .transpose(0, 2, 1, 3)
        .reshape(frame_count, pixels // 4, lat_channels * 4)
    )
    width = w_in.shape[1]
    embed = time_embed(step_index, width)
    block_rows = patches.shape[1]
    summed = (
        jnp.dot(patches.reshape(-1, patches.shape[2]), w_in, preferred_element_type=jnp.float32)
        + embed
    )
    tokens = lax.all_gather(
        rms_scale(summed, norm_gain).astype(jnp.bfloat16).reshape(frame_count, block_rows, width),
        "grp",
        axis=1,
        tiled=True,
    ).reshape(-1, width)
    history = jnp.zeros((hist.shape[0], width), jnp.float32)
    for level in range(3):
        history = (
            history
            + jnp.dot(hist, w_hist[level], preferred_element_type=jnp.float32)
            * (hist_level == level).astype(jnp.float32)[:, None]
        )
    history = rms_scale(history, norm_gain).astype(jnp.bfloat16)
    both_rows = jnp.concatenate([tokens, history], axis=0)
    sec_rows = tokens.shape[0]
    key_rows = both_rows.shape[0]
    head_size = q_gain.shape[0]
    heads_local = w_query.shape[1] // head_size
    query = rms_scale(
        jnp.dot(tokens, w_query, preferred_element_type=jnp.float32).reshape(
            sec_rows, heads_local, head_size
        ),
        q_gain,
    ).astype(jnp.bfloat16)
    flattened_keys = (
        rms_scale(
            jnp.dot(both_rows, w_key, preferred_element_type=jnp.float32).reshape(
                key_rows, heads_local, head_size
            ),
            k_gain,
        )
        .astype(jnp.bfloat16)
        .reshape(key_rows, heads_local * head_size)
    )
    values_flat = jnp.dot(both_rows, w_value, preferred_element_type=jnp.float32).astype(
        jnp.bfloat16
    )
    seq_count = lax.axis_size("seq")
    shard_ids = jnp.arange(seq_count, dtype=jnp.int32)
    scale = 1.0 / math.sqrt(head_size)
    run_max = jnp.full((heads_local, sec_rows), -1e30, jnp.float32)
    key_piece = lax.all_gather(flattened_keys, "seq", axis=0, tiled=True)
    value_piece = lax.all_gather(values_flat, "seq", axis=0, tiled=True)
    count_rows = key_piece.shape[0]
    row_index = jnp.arange(count_rows, dtype=jnp.int32)
    owner = row_index // key_rows
    local_index = row_index - owner * key_rows
    owner_count = jnp.sum(
        jnp.where(owner[:, None] == shard_ids[None, :], hist_count[None, :], 0), axis=1
    )
    alive = (local_index < sec_rows) | (local_index - sec_rows < owner_count)
    key_heads = key_piece.reshape(count_rows, heads_local, head_size)
    value_heads = value_piece.reshape(count_rows, heads_local, head_size)
    scores = (
        jnp.einsum("qhd,khd->hqk", query, key_heads, preferred_element_type=jnp.float32) * scale
    )
    scores = jnp.where(alive[None, None, :], scores, -1e30)
    new_max = jnp.maximum(run_max, jnp.max(scores, axis=-1))
    soft = jnp.where(alive[None, None, :], jnp.exp(scores - new_max[..., None]), 0.0)
    new_sum = jnp.sum(soft, axis=-1)
    new_weighted = jnp.einsum(
        "hqk,khd->hqd", soft.astype(jnp.bfloat16), value_heads, preferred_element_type=jnp.float32
    )
    attended = new_weighted / new_sum[..., None]
    heads_out = (
        attended.astype(jnp.bfloat16).transpose(1, 0, 2).reshape(sec_rows, heads_local * head_size)
    )
    partial_out = jnp.dot(heads_out, w_out, preferred_element_type=jnp.float32)
    return lax.psum_scatter(
        partial_out.astype(jnp.bfloat16), "grp", scatter_dimension=1, tiled=True
    )


def solution(mesh):
    placed = (
        P("seq", None, "grp"),
        P(),
        P(),
        P(),
        P("seq", None, "grp"),
        P(),
        P("seq", None),
        P("seq"),
        P(),
        P(),
        P(),
        P(),
        P(None, "grp"),
        P(None, "grp"),
        P(None, "grp"),
        P(),
        P(),
        P("grp", None),
    )
    return jax.shard_map(
        local, mesh=mesh, in_specs=placed, out_specs=P("seq", "grp"), check_vma=False
    )
```

profile of v0, /device:TPU:1, one launch (start us, length us, event | category | flops | bytes accessed | tf_op | source)
XLA Modules:
  0.0 367.8 jit_solution(9510496227103605106)
XLA Ops:
  6.6 4.7 %collective-permute-start = (bf16[2,128,192]{1,2,0:T(8,128)(2,1)}, bf16[2,128,192]{1,2,0:T(8,128)(2,1)S(1)}, u32[]{:S(2)}, u32[]{:S(2)}) collective-permute-start(bf16[2,128,192]{1,2,0:T(8,128)(2,1)} %param.18), channel_id=1, source_target_pairs={{0,1},{1,2},{2,3},{3,4},{4,5},{5,6},{6,7},{7,8},{8,9},{9,10},{10,1... | collective-permute-start | bytes 294920 | tf_op jit(solution)/shard_map/ppermute | solution.py:14
  12.0 1.1 fusion.51
  13.1 0.7 compare_convert_fusion
  13.8 1.2 convolution_multiply_fusion.2
  14.9 1.2 fusion.7
  16.2 1.0 convolution_add_fusion.2
  17.1 1.1 fusion.24
  19.1 1.0 multiply_convert_fusion
  20.2 1.3 multiply_reduce_fusion.2
  21.6 25.8 %all-gather.4.cloned.1.call-done = bf16[2,96,3072]{2,1,0:T(8,128)(2,1)} async-done(((bf16[2,48,3072]{2,1,0:T(8,128)(2,1)}), bf16[2,96,3072]{2,1,0:T(8,128)(2,1)}) %all-gather.4.cloned.1.call-update) | async-done | bytes 1179664 | tf_op jit(solution)/shard_map/all_gather | solution.py:76
  47.3 3.8 %fusion.67 = (f32[200,768]{1,0:T(8,128)S(1)}, f32[200,768]{1,0:T(8,128)S(1)}) fusion(bf16[3072,768]{1,0:T(8,128)(2,1)} %param.31, bf16[8,3072]{1,0:T(8,128)(2,1)S(1)} %multiply_convert_fusion.4, bf16[192,3072]{1,0:T(8,128)(2,1)} %bitcast.98), kind=kOutput, calls=%fused_computation.95 | convolution fusion | flops 946329600 | bytes 7176192 | tf_op jit(solution)/shard_map/dot_general | solution.py:103
  52.1 0.9 fusion.27
  53.1 4.6 %convolution_convert_fusion.1 = bf16[200,768]{1,0:T(8,128)(2,1)} fusion(bf16[3072,768]{1,0:T(8,128)(2,1)} %param.32, bf16[8,3072]{1,0:T(8,128)(2,1)S(1)} %multiply_convert_fusion.4, bf16[192,3072]{1,0:T(8,128)(2,1)} %bitcast.99), kind=kOutput, calls=%fused_computation.18 | convolution fusion | flops 946329600 | bytes 6254592 | tf_op jit(solution)/shard_map/dot_general | solution.py:111
  57.9 6.7 %copy.49 = bf16[3072,768]{0,1:T(8,128)(2,1)} copy(bf16[3072,768]{1,0:T(8,128)(2,1)} %param.30) | data formatting | bytes 9437184 | tf_op args[12]
  65.3 4.3 %multiply_reduce_fusion.1 = (f32[192,6]{0,1:T(8,128)S(1)}, f32[192,6,128]{2,0,1:T(8,128)S(1)}) fusion(bf16[192,3072,1]{1,0,2:T(8,128)(2,1)S(1)} %bitcast.100, bf16[6,128,3072]{2,1,0:T(8,128)(2,1)} %bitcast.93), kind=kOutput, calls=%fused_computation.37 | convolution fusion | flops 906263424 | bytes 6492672 | tf_op jit(solution)/shard_map/dot_general | solution.py:96
  69.6 99.2 %all-gather.6.cloned.1.call-done = bf16[12800,768]{1,0:T(8,128)(2,1)} async-done(((bf16[200,768]{1,0:T(8,128)(2,1)}), bf16[12800,768]{1,0:T(8,128)(2,1)}) %all-gather.6.cloned.1.call-update) | async-done | bytes 19660816 | tf_op jit(solution)/shard_map/all_gather | solution.py:118
  168.8 23.8 %copy.52 = bf16[12800,768]{0,1:T(8,128)(2,1)} copy(bf16[12800,768]{1,0:T(8,128)(2,1)} %all-gather.6.cloned.1.call-done) | data formatting | bytes 39321600 | tf_op jit(solution)/shard_map/all_gather | solution.py:118
  192.7 27.5 %fusion = (f32[6,192]{1,0:T(8,128)S(1)}, f32[6,192,12800]{2,1,0:T(8,128)}) fusion(pred[12800]{0:T(1024)(128)(4,1)S(1)} %fusion.46, bf16[12800,6,128]{0,2,1:T(8,128)(2,1)} %bitcast.91, f32[192,6,128]{2,0,1:T(8,128)S(1)} %get-tuple-element.15, f32[128]{0:T(128)S(1)} %copy-done.4, f32[192,6]{0,1:T(8,128)S(1)} %add_rsqrt_fusion.1), kind=kOutput, calls=%fused_computation.2 | convolution fusion | flops 3819551744 | bytes 79255552 | tf_op jit(solution)/shard_map/qhd,khd->hqk/dot_general | solution.py:131
  220.1 21.5 %fusion.1 = f32[6,192]{1,0:T(8,128)S(1)} fusion(f32[6,192,12800]{2,1,0:T(8,128)} %get-tuple-element.17, f32[6,192]{1,0:T(8,128)S(1)} %broadcast_maximum_fusion, pred[12800]{0:T(1024)(128)(4,1)S(1)} %fusion.46), kind=kLoop, calls=%fused_computation.3 | loop fusion | flops 73726848 | bytes 59004416 | tf_op jit(solution)/shard_map/reduce_sum | solution.py:136
  241.6 42.6 %all-gather.8.cloned.1.call-done = bf16[12800,768]{1,0:T(8,128)(2,1)} async-done(((bf16[200,768]{1,0:T(8,128)(2,1)}), bf16[12800,768]{1,0:T(8,128)(2,1)}) %all-gather.8.cloned.1.call-update) | async-done | bytes 19660816 | tf_op jit(solution)/shard_map/all_gather | solution.py:119
  284.2 23.8 %copy.54 = bf16[12800,768]{0,1:T(8,128)(2,1)} copy(bf16[12800,768]{1,0:T(8,128)(2,1)} %all-gather.8.cloned.1.call-done) | data formatting | bytes 39321600 | tf_op jit(solution)/shard_map/all_gather | solution.py:119
  308.0 27.0 %fusion.17 = bf16[6,24,8,128]{3,2,1,0:T(8,128)(2,1)S(1)} fusion(bf16[12800,6,128]{0,2,1:T(8,128)(2,1)} %bitcast.92, f32[6,192,12800]{2,1,0:T(8,128)} %get-tuple-element.17, f32[6,192]{1,0:T(8,128)S(1)} %broadcast_maximum_fusion, pred[12800]{0:T(1024)(128)(4,1)S(1)} %fusion.46, f32[192,6]{0,1:T(8,128)S(1)} %bitcast.97), kind=kOutput, calls=%fused_computation.23 | convolution fusion | flops 3848896512 | bytes 78960128 | tf_op jit(solution)/shard_map/hqk,khd->hqd/dot_general | solution.py:137
  335.1 4.5 %convolution_convert_fusion = bf16[192,3072]{1,0:T(8,128)(2,1)} fusion(bf16[768,3072]{1,0:T(8,128)(2,1)} %param.35, bf16[6,24,8,128]{3,2,1,0:T(8,128)(2,1)S(1)} %fusion.17), kind=kOutput, calls=%fused_computation.7 | convolution fusion | flops 906559488 | bytes 6193152 | tf_op jit(solution)/shard_map/dot_general | solution.py:144
  339.6 21.7 %reduce-scatter.2.cloned.1.call-done = bf16[192,1536]{1,0:T(8,128)(2,1)} async-done(((bf16[192,3072]{1,0:T(8,128)(2,1)}), bf16[192,1536]{1,0:T(8,128)(2,1)}) %reduce-scatter.2.cloned.1.call-update) | async-done | bytes 589840 | tf_op jit(solution)/shard_map/reduce_scatter | solution.py:145
  (46 shorter events, 2.9 us)
Async XLA Ops:
  6.5 12.1 %copy-start = (bf16[64,3072]{1,0:T(8,128)(2,1)S(1)}, bf16[64,3072]{1,0:T(8,128)(2,1)}, u32[]{:S(2)}) copy-start(bf16[64,3072]{1,0:T(8,128)(2,1)} %param.27) | copy-start | bytes 1179652
  6.5 13.6 %copy-start.3 = (bf16[8,64]{1,0:T(8,128)(2,1)S(1)}, bf16[8,64]{1,0:T(8,128)(2,1)}, u32[]{:S(2)}) copy-start(bf16[8,64]{1,0:T(8,128)(2,1)} %param.24) | copy-start | bytes 3076
  6.5 12.5 %copy-start.2 = (f32[3072]{0:T(1024)S(1)}, f32[3072]{0:T(1024)}, u32[]{:S(2)}) copy-start(f32[3072]{0:T(1024)} %param.29) | copy-start | bytes 36868
  6.5 14.9 %copy-start.6 = (f32[128]{0:T(128)S(1)}, f32[128]{0:T(128)}, u32[]{:S(2)}) copy-start(f32[128]{0:T(128)} %param.34) | copy-start | bytes 1540
  6.5 40.8 %all-gather.4.cloned.1.call-start = ((), (), s32[]{:S(2)}) async-start(), calls=%async_computation.1 | async-start | bytes 1769472 | tf_op jit(solution)/shard_map/all_gather | solution.py:76
  6.6 9.6 %collective-permute-start = (bf16[2,128,192]{1,2,0:T(8,128)(2,1)}, bf16[2,128,192]{1,2,0:T(8,128)(2,1)S(1)}, u32[]{:S(2)}, u32[]{:S(2)}) collective-permute-start(bf16[2,128,192]{1,2,0:T(8,128)(2,1)} %param.18), channel_id=1, source_target_pairs={{0,1},{1,2},{2,3},{3,4},{4,5},{5,6},{6,7},{7,8},{8,9},{9,10},{10,1... | collective-permute-start | bytes 294920 | tf_op jit(solution)/shard_map/ppermute | solution.py:14
  20.1 148.7 %all-gather.6.cloned.1.call-start = ((), (), s32[]{:S(2)}) async-start(), calls=%async_computation.2 | async-start | bytes 19968000 | tf_op jit(solution)/shard_map/all_gather | solution.py:118
  53.0 231.2 %all-gather.8.cloned.1.call-start = ((), (), s32[]{:S(2)}) async-start(), calls=%async_computation.3 | async-start | bytes 19968000 | tf_op jit(solution)/shard_map/all_gather | solution.py:119
  57.6 7.0 %copy-start.5 = (s32[64]{0:T(128)S(1)}, s32[64]{0:T(128)}, u32[]{:S(2)}) copy-start(s32[64]{0:T(128)} %param.26) | copy-start | bytes 772
  57.7 7.6 %copy-start.7 = (bf16[2,96,3072]{2,1,0:T(8,128)(2,1)S(1)}, bf16[2,96,3072]{2,1,0:T(8,128)(2,1)}, u32[]{:S(2)}) copy-start(bf16[2,96,3072]{2,1,0:T(8,128)(2,1)} %all-gather.4.cloned.1.call-done) | copy-start | bytes 3538948
  57.7 303.6 %reduce-scatter.2.cloned.1.call-start = ((), (), s32[]{:S(2)}) async-start(), calls=%async_computation.4 | async-start | bytes 1769472 | tf_op jit(solution)/shard_map/reduce_scatter | solution.py:145
  69.6 123.1 %copy-start.4 = (f32[128]{0:T(128)S(1)}, f32[128]{0:T(128)}, u32[]{:S(2)}) copy-start(f32[128]{0:T(128)} %param.33) | copy-start | bytes 1540
  308.0 53.3 %copy-start.1 = (bf16[64,3072]{1,0:T(8,128)(2,1)S(1)}, bf16[64,3072]{1,0:T(8,128)(2,1)}, u32[]{:S(2)}) copy-start(bf16[64,3072]{1,0:T(8,128)(2,1)} %param.27) | copy-start | bytes 1179652
Sparse Core Ops, SparseCore 0:
  20.2 27.0 all-gather.3
  53.1 115.6 all-gather.5
  172.0 112.1 all-gather.7
  339.7 21.5 reduce-scatter.1
where the time goes:
time: 370 us; the launch traced here: 368 us
  waiting for transfers between devices  189 us (51%)
  matrix products  78.8 us (21%)
  local copies, waits for them, and re-layouts  55.3 us (15%)
  other arithmetic  25.1 us (7%)
  between operations  14 us (4%)
  starting transfers between devices  5.07 us (1%)
    all_gather x1, waiting for transfers between devices, local(): key_piece = lax.all_gather(flattened_keys, 'seq', axis=0, tiled=True)  99.2 us
    all_gather x1, waiting for transfers between devices, local(): value_piece = lax.all_gather(values_flat, 'seq', axis=0, tiled=True)  42.6 us
    dot_general x1, matrix products, local(): jnp.einsum('qhd,khd->hqk', query, key_heads, preferred_element_type=jnp.f...  27.5 us
    dot_general x1, matrix products, local(): jnp.einsum('hqk,khd->hqd', soft.astype(jnp.bfloat16), value_heads, prefer...  27 us
    all_gather x1, waiting for transfers between devices, local(): lax.all_gather(rms_scale(summed, norm_gain).astype(jnp.bfloat16).reshape(...  25.8 us
    all_gather x1, local copies, waits for them, and re-layouts, local(): key_piece = lax.all_gather(flattened_keys, 'seq', axis=0, tiled=True)  23.8 us
    all_gather x1, local copies, waits for them, and re-layouts, local(): value_piece = lax.all_gather(values_flat, 'seq', axis=0, tiled=True)  23.8 us
    reduce_scatter x1, waiting for transfers between devices, local(): lax.psum_scatter(partial_out.astype(jnp.bfloat16), 'grp', scatter_dimensi...  21.7 us
  transfers between devices with their start and end apart: 5, of which 4 were waited for; matrix products, arithmetic and copies ran while one was open for 26% of the time, Pallas kernels for 0%

commit v1 on v0

--- a/solution.py
+++ b/solution.py
@@ -115,8 +115,13 @@
     shard_ids = jnp.arange(seq_count, dtype=jnp.int32)
     scale = 1.0 / math.sqrt(head_size)
     run_max = jnp.full((heads_local, sec_rows), -1e30, jnp.float32)
-    key_piece = lax.all_gather(flattened_keys, "seq", axis=0, tiled=True)
-    value_piece = lax.all_gather(values_flat, "seq", axis=0, tiled=True)
+    key_piece, value_piece = jnp.split(
+        lax.all_gather(
+            jnp.concatenate([flattened_keys, values_flat], axis=1), "seq", axis=0, tiled=True
+        ),
+        [flattened_keys.shape[1]],
+        axis=1,
+    )
     count_rows = key_piece.shape[0]
     row_index = jnp.arange(count_rows, dtype=jnp.int32)
     owner = row_index // key_rows

time: 370 us -> 417 us (1.13)
  local copies, waits for them, and re-layouts: 55.3 us -> 82.4 us
  waiting for transfers between devices: 189 us -> 214 us
    split x0 -> x3, local copies, waits for them, and re-layouts: none -> 74.7 us  [local(): jnp.split(lax.all_gather(jnp.concatenate([flattened_keys, values_flat], a...]
    all_gather x2 -> x0, local copies, waits for them, and re-layouts: 47.6 us -> none  [the longest x1 23.8 us: local(): key_piece = lax.all_gather(flattened_keys, 'seq', axis=0, tiled=True)]
    all_gather x2 -> x1, waiting for transfers between devices: 142 us -> 166 us  [local(): lax.all_gather(jnp.concatenate([flattened_keys, values_flat], axis=1), 's...]
  transfers between devices with their start and end apart: 5 -> 4, of which waited for: 4 -> 3; matrix products, arithmetic and copies ran while one was open for 26% -> 4% of each run, Pallas kernels for 0% -> 0%
where the time goes in v1:
time: 417 us; the launch traced here: 416 us
  waiting for transfers between devices  214 us (51%)
  local copies, waits for them, and re-layouts  82.4 us (20%)
  matrix products  77.3 us (19%)
  other arithmetic  23 us (6%)
  between operations  14 us (3%)
  starting transfers between devices  5.02 us (1%)
    all_gather x1, waiting for transfers between devices, local(): lax.all_gather(jnp.concatenate([flattened_keys, values_flat], axis=1), 's...  166 us
    split x3, local copies, waits for them, and re-layouts, local(): jnp.split(lax.all_gather(jnp.concatenate([flattened_keys, values_flat], a...  74.7 us
    dot_general x1, matrix products, local(): jnp.einsum('hqk,khd->hqd', soft.astype(jnp.bfloat16), value_heads, prefer...  27 us
    dot_general x1, matrix products, local(): jnp.einsum('qhd,khd->hqk', query, key_heads, preferred_element_type=jnp.f...  27 us
    all_gather x1, waiting for transfers between devices, local(): lax.all_gather(rms_scale(summed, norm_gain).astype(jnp.bfloat16).reshape(...  25.8 us
    reduce_scatter x1, waiting for transfers between devices, local(): lax.psum_scatter(partial_out.astype(jnp.bfloat16), 'grp', scatter_dimensi...  21.7 us
    reduce_sum x1, other arithmetic, local(): new_sum = jnp.sum(soft, axis=-1)  19.2 us
  transfers between devices with their start and end apart: 4, of which 3 were waited for; matrix products, arithmetic and copies ran while one was open for 4% of the time, Pallas kernels for 0%

profile of v1, /device:TPU:1, one launch (start us, length us, event | category | flops | bytes accessed | tf_op | source)
XLA Modules:
  0.0 415.6 jit_solution(3678934692640621613)
XLA Ops:
  6.6 4.7 %collective-permute-start = (bf16[2,128,192]{1,2,0:T(8,128)(2,1)}, bf16[2,128,192]{1,2,0:T(8,128)(2,1)S(1)}, u32[]{:S(2)}, u32[]{:S(2)}) collective-permute-start(bf16[2,128,192]{1,2,0:T(8,128)(2,1)} %param.18), channel_id=1, source_target_pairs={{0,1},{1,2},{2,3},{3,4},{4,5},{5,6},{6,7},{7,8},{8,9},{9,10},{10,1... | collective-permute-start | bytes 294920 | tf_op jit(solution)/shard_map/ppermute | solution.py:14
  12.0 0.7 compare_convert_fusion
  12.7 1.1 fusion.51
  13.8 1.2 convolution_multiply_fusion.2
  14.9 1.2 fusion.7
  16.2 1.0 convolution_add_fusion.2
  17.1 1.1 fusion.24
  19.1 1.0 multiply_convert_fusion
  20.2 1.3 multiply_reduce_fusion.2
  21.6 25.8 %all-gather.3.cloned.1.call-done = bf16[2,96,3072]{2,1,0:T(8,128)(2,1)} async-done(((bf16[2,48,3072]{2,1,0:T(8,128)(2,1)}), bf16[2,96,3072]{2,1,0:T(8,128)(2,1)}) %all-gather.3.cloned.1.call-update) | async-done | bytes 1179664 | tf_op jit(solution)/shard_map/all_gather | solution.py:76
  47.3 3.9 convolution_convert_fusion.1
  51.3 3.5 fusion.68
  55.9 0.9 pad_maximum_fusion.3
  57.0 6.8 %copy.49 = bf16[3072,768]{0,1:T(8,128)(2,1)} copy(bf16[3072,768]{1,0:T(8,128)(2,1)} %param.30) | data formatting | bytes 9437184 | tf_op args[12]
  64.5 4.2 %multiply_reduce_fusion.1 = (f32[192,6]{0,1:T(8,128)S(1)}, f32[192,6,128]{2,0,1:T(8,128)S(1)}) fusion(bf16[192,3072,1]{1,0,2:T(8,128)(2,1)S(1)} %bitcast.100, bf16[6,128,3072]{2,1,0:T(8,128)(2,1)} %bitcast.93), kind=kOutput, calls=%fused_computation.38 | convolution fusion | flops 906263424 | bytes 6492672 | tf_op jit(solution)/shard_map/dot_general | solution.py:96
  68.7 166.2 %all-gather.5.cloned.1.call-done = bf16[12800,1536]{1,0:T(8,128)(2,1)} async-done(((bf16[200,1536]{1,0:T(8,128)(2,1)}), bf16[12800,1536]{1,0:T(8,128)(2,1)}) %all-gather.5.cloned.1.call-update) | async-done | bytes 39321616 | tf_op jit(solution)/shard_map/all_gather | solution.py:119
  234.9 26.9 %fusion.67 = (bf16[12800,768]{1,0:T(8,128)(2,1)}, bf16[12800,768]{1,0:T(8,128)(2,1)}) fusion(bf16[12800,1536]{1,0:T(8,128)(2,1)} %all-gather.5.cloned.1.call-done), kind=kLoop, calls=%fused_computation.96 | loop fusion | bytes 78643200 | tf_op jit(solution)/shard_map/split | solution.py:118
  261.8 23.9 %copy.52 = bf16[12800,768]{0,1:T(8,128)(2,1)} copy(bf16[12800,768]{1,0:T(8,128)(2,1)} %get-tuple-element.5) | data formatting | bytes 39321600 | tf_op jit(solution)/shard_map/split | solution.py:118
  285.7 23.9 %copy.54 = bf16[12800,768]{0,1:T(8,128)(2,1)} copy(bf16[12800,768]{1,0:T(8,128)(2,1)} %get-tuple-element.6) | data formatting | bytes 39321600 | tf_op jit(solution)/shard_map/split | solution.py:118
  309.6 27.0 %fusion = (f32[6,192]{1,0:T(8,128)S(1)}, f32[6,192,12800]{2,1,0:T(8,128)}) fusion(pred[12800]{0:T(1024)(128)(4,1)S(1)} %fusion.46, bf16[12800,6,128]{0,2,1:T(8,128)(2,1)} %bitcast.91, f32[192,6,128]{2,0,1:T(8,128)S(1)} %get-tuple-element.17, f32[128]{0:T(128)S(1)} %copy-done.4, f32[192,6]{0,1:T(8,128)S(1)} %add_rsqrt_fusion.1), kind=kOutput, calls=%fused_computation.2 | convolution fusion | flops 3819551744 | bytes 79255552 | tf_op jit(solution)/shard_map/qhd,khd->hqk/dot_general | solution.py:136
  336.6 19.2 %fusion.1 = f32[6,192]{1,0:T(8,128)S(1)} fusion(f32[6,192,12800]{2,1,0:T(8,128)} %get-tuple-element.19, f32[6,192]{1,0:T(8,128)S(1)} %broadcast_maximum_fusion, pred[12800]{0:T(1024)(128)(4,1)S(1)} %fusion.46), kind=kLoop, calls=%fused_computation.3 | loop fusion | flops 73726848 | bytes 59004416 | tf_op jit(solution)/shard_map/reduce_sum | solution.py:141
  355.8 27.0 %fusion.17 = bf16[6,24,8,128]{3,2,1,0:T(8,128)(2,1)S(1)} fusion(bf16[12800,6,128]{0,2,1:T(8,128)(2,1)} %bitcast.92, f32[6,192,12800]{2,1,0:T(8,128)} %get-tuple-element.19, f32[6,192]{1,0:T(8,128)S(1)} %broadcast_maximum_fusion, pred[12800]{0:T(1024)(128)(4,1)S(1)} %fusion.46, f32[192,6]{0,1:T(8,128)S(1)} %bitcast.97), kind=kOutput, calls=%fused_computation.23 | convolution fusion | flops 3848896512 | bytes 78960128 | tf_op jit(solution)/shard_map/hqk,khd->hqd/dot_general | solution.py:142
  382.9 4.5 %convolution_convert_fusion = bf16[192,3072]{1,0:T(8,128)(2,1)} fusion(bf16[768,3072]{1,0:T(8,128)(2,1)} %param.35, bf16[6,24,8,128]{3,2,1,0:T(8,128)(2,1)S(1)} %fusion.17), kind=kOutput, calls=%fused_computation.7 | convolution fusion | flops 906559488 | bytes 6193152 | tf_op jit(solution)/shard_map/dot_general | solution.py:149
  387.3 21.7 %reduce-scatter.2.cloned.1.call-done = bf16[192,1536]{1,0:T(8,128)(2,1)} async-done(((bf16[192,3072]{1,0:T(8,128)(2,1)}), bf16[192,1536]{1,0:T(8,128)(2,1)}) %reduce-scatter.2.cloned.1.call-update) | async-done | bytes 589840 | tf_op jit(solution)/shard_map/reduce_scatter | solution.py:150
  (47 shorter events, 3.0 us)
Async XLA Ops:
  6.5 12.1 %copy-start = (bf16[64,3072]{1,0:T(8,128)(2,1)S(1)}, bf16[64,3072]{1,0:T(8,128)(2,1)}, u32[]{:S(2)}) copy-start(bf16[64,3072]{1,0:T(8,128)(2,1)} %param.27) | copy-start | bytes 1179652
  6.5 13.6 %copy-start.3 = (bf16[8,64]{1,0:T(8,128)(2,1)S(1)}, bf16[8,64]{1,0:T(8,128)(2,1)}, u32[]{:S(2)}) copy-start(bf16[8,64]{1,0:T(8,128)(2,1)} %param.24) | copy-start | bytes 3076
  6.5 12.5 %copy-start.2 = (f32[3072]{0:T(1024)S(1)}, f32[3072]{0:T(1024)}, u32[]{:S(2)}) copy-start(f32[3072]{0:T(1024)} %param.29) | copy-start | bytes 36868
  6.5 14.9 %copy-start.6 = (f32[128]{0:T(128)S(1)}, f32[128]{0:T(128)}, u32[]{:S(2)}) copy-start(f32[128]{0:T(128)} %param.34) | copy-start | bytes 1540
  6.5 40.8 %all-gather.3.cloned.1.call-start = ((), (), s32[]{:S(2)}) async-start(), calls=%async_computation.1 | async-start | bytes 1769472 | tf_op jit(solution)/shard_map/all_gather | solution.py:76
  6.6 9.6 %collective-permute-start = (bf16[2,128,192]{1,2,0:T(8,128)(2,1)}, bf16[2,128,192]{1,2,0:T(8,128)(2,1)S(1)}, u32[]{:S(2)}, u32[]{:S(2)}) collective-permute-start(bf16[2,128,192]{1,2,0:T(8,128)(2,1)} %param.18), channel_id=1, source_target_pairs={{0,1},{1,2},{2,3},{3,4},{4,5},{5,6},{6,7},{7,8},{8,9},{9,10},{10,1... | collective-permute-start | bytes 294920 | tf_op jit(solution)/shard_map/ppermute | solution.py:14
  20.1 214.8 %all-gather.5.cloned.1.call-start = ((), (), s32[]{:S(2)}) async-start(), calls=%async_computation.2 | async-start | bytes 39936000 | tf_op jit(solution)/shard_map/all_gather | solution.py:119
  47.3 3.9 copy-start.7
  56.8 7.1 %copy-start.5 = (s32[64]{0:T(128)S(1)}, s32[64]{0:T(128)}, u32[]{:S(2)}) copy-start(s32[64]{0:T(128)} %param.26) | copy-start | bytes 772
  56.8 7.7 %copy-start.8 = (bf16[2,96,3072]{2,1,0:T(8,128)(2,1)S(1)}, bf16[2,96,3072]{2,1,0:T(8,128)(2,1)}, u32[]{:S(2)}) copy-start(bf16[2,96,3072]{2,1,0:T(8,128)(2,1)} %all-gather.3.cloned.1.call-done) | copy-start | bytes 3538948
  56.8 352.2 %reduce-scatter.2.cloned.1.call-start = ((), (), s32[]{:S(2)}) async-start(), calls=%async_computation.3 | async-start | bytes 1769472 | tf_op jit(solution)/shard_map/reduce_scatter | solution.py:150
  285.7 23.9 %copy-start.4 = (f32[128]{0:T(128)S(1)}, f32[128]{0:T(128)}, u32[]{:S(2)}) copy-start(f32[128]{0:T(128)} %param.33) | copy-start | bytes 1540
  355.8 53.2 %copy-start.1 = (bf16[64,3072]{1,0:T(8,128)(2,1)S(1)}, bf16[64,3072]{1,0:T(8,128)(2,1)}, u32[]{:S(2)}) copy-start(bf16[64,3072]{1,0:T(8,128)(2,1)} %param.27) | copy-start | bytes 1179652
Sparse Core Ops, SparseCore 0:
  20.2 27.0 all-gather.2
  56.9 177.9 all-gather.4
  387.5 21.5 reduce-scatter.1
